TPU v7x, 32 devices: a whole 2x2x4 slice. The times are simulated.
32 devices in a mesh: px: 4 (over x, core), py: 8 (over z, y).
Axes of the slice: x: 2, y: 2, z: 4, core: 2. Of those that a mesh axis runs over, the one named last changes fastest.
Arguments:
- fraction: float32 [32, 64, 640], P('px', 'py'), may hold values from 0 to 1
- courant_x: float32 [32, 64, 640], P('px', 'py'), may hold values from -0.5 to 0.5
- courant_y: float32 [32, 64, 640], P('px', 'py'), may hold values from -0.5 to 0.5
- courant_z: float32 [32, 64, 640], P('px', 'py'), may hold values from -0.5 to 0.5
- labels: int32 [32, 64, 640], P('px', 'py'), may hold values from -1 to 31, as said below
- structure_owner: int32 [4, 32], P('px'), may hold values from 0 to 7, as said below
- parcel_owner: int32 [4, 32], P('px'), may hold values from 0 to 7, as said below
Outputs:
- remaining: float32 [32, 64, 640], P('px', 'py')
- moments: float32 [4, 13, 32], P('px', None, 'py')
- parcels: float32 [4, 13, 32], P('px', None, 'py')
Inputs may be any that keep to these rules, and one draw needn't show every extreme that they name: `labels`: a label names a structure of the cell's row. `structure_owner`: in each row every index of py owns exactly 4 structures. `parcel_owner`: in each row every index of py receives exactly 4 parcels.
All inputs are finite; a program needn't handle non-finite values.
Results may differ from a plain program's by a relative error of at most 0.0003.
Values sent between devices are 32-bit elements; how exact they have to be, the bound alone decides.
A program may use at most 64 MiB of HBM per device.

v0:
```python
import math

import jax
import jax.numpy as jnp
from jax import lax
from jax.sharding import PartitionSpec as P


def with_halo(x, sides, width, wrap):
    for axis, dim in sides:
        size, length = (lax.axis_size(axis), x.shape[dim])
        up = [(i, (i + 1) % size) for i in range(size if wrap else size - 1)]
        down = [(j, i) for i, j in up]
        last = lax.slice_in_dim(x, length - width, length, axis=dim)
        initial = lax.slice_in_dim(x, 0, width, axis=dim)
        before = lax.ppermute(last, axis, up)
        after = lax.ppermute(initial, axis, down)
        x = jnp.concatenate([before, x, after], axis=dim)
    return x


def advance(padded_frac, padded_cour, length, axis):

    def part(array, start, count):
        return lax.slice_in_dim(array, start, start + count, axis=axis)

    centre = part(padded_frac, 1, length + 2)
    spread = 0.5 * (part(padded_frac, 2, length + 2) - part(padded_frac, 0, length + 2))
    bound = 2.0 * jnp.minimum(centre, 1.0 - centre)
    slope = jnp.minimum(jnp.maximum(spread, -bound), bound)
    courant = part(padded_cour, 1, length + 1)
    upwind = part(centre, 0, length + 1) + 0.5 * (1.0 - courant) * part(slope, 0, length + 1)
    downwind = part(centre, 1, length + 1) - 0.5 * (1.0 + courant) * part(slope, 1, length + 1)
    flux = courant * jnp.where(courant > 0.0, upwind, downwind)
    middle = part(padded_frac, 2, length)
    high = part(courant, 1, length)
    low = part(courant, 0, length)
    updated = middle - (part(flux, 1, length) - part(flux, 0, length)) + middle * (high - low)
    return (updated, 0.5 * (high + low))


def parcel_rows(moment_rows):
    volume = moment_rows[0]
    safe = jnp.maximum(volume, 0.5)
    centre = moment_rows[1:4] / safe
    velocity = moment_rows[4:7] / safe
    square = moment_rows[7:10] / safe - centre * centre
    cross = jnp.stack(
        [
            moment_rows[10] / safe - centre[0] * centre[1],
            moment_rows[11] / safe - centre[0] * centre[2],
            moment_rows[12] / safe - centre[1] * centre[2],
        ]
    )
    return jnp.concatenate([volume[None], centre, velocity, square, cross], 0)


def slot_table(owner_row, per_owner):
    count = owner_row.shape[0]
    index = jnp.arange(count, dtype=jnp.int32)
    same = owner_row[:, None] == owner_row[None, :]
    earlier = index[None, :] < index[:, None]
    rank = jnp.sum((same & earlier).astype(jnp.int32), axis=1)
    position = owner_row * per_owner + rank
    return (position[:, None] == index[None, :]).astype(jnp.float32)


def product(left, right):
    return jnp.dot(left, right, precision=lax.Precision.HIGHEST, preferred_element_type=jnp.float32)


def local(fraction, courant_x, courant_y, courant_z, labels, structure_owner, parcel_owner):
    rows_x, rows_y, depth = fraction.shape
    padded = with_halo(jnp.stack([fraction, courant_x]), (("px", 1),), 2, True)
    first, velocity_x = advance(padded[0], padded[1], rows_x, 0)
    padded_y = with_halo(jnp.stack([first, courant_y]), (("py", 2),), 2, False)
    second, velocity_y = advance(padded_y[0], padded_y[1], rows_y, 1)
    pad_z = ((0, 0), (0, 0), (2, 2))
    third, velocity_z = advance(jnp.pad(second, pad_z), jnp.pad(courant_z, pad_z), depth, 2)
    remaining = jnp.where(labels >= 0, jnp.float32(0.0), third)
    width_py = lax.axis_size("py")
    row_index = lax.axis_index("py")
    total_x = rows_x * lax.axis_size("px")
    total_y = rows_y * width_py
    structures = structure_owner.shape[1]
    per_owner = structures // width_py
    scale = 4.0 / (rows_x * rows_y * rows_y)
    start_x = lax.axis_index("px") * rows_x
    start_y = row_index * rows_y
    coord_x = ((start_x + jnp.arange(rows_x, dtype=jnp.int32)).astype(jnp.float32) + 0.5)[
        :, None, None
    ] / total_x
    coord_y = ((start_y + jnp.arange(rows_y, dtype=jnp.int32)).astype(jnp.float32) + 0.5)[
        None, :, None
    ] / total_y
    coord_z = (jnp.arange(depth, dtype=jnp.int32).astype(jnp.float32) + 0.5)[None, None, :] / depth
    weight = third * scale
    shape = weight.shape
    cells = rows_x * rows_y * depth
    block = math.gcd(cells, 4096)
    blocks = cells // block
    pieces = [
        jnp.ones(shape, jnp.float32),
        coord_x,
        coord_y,
        coord_z,
        velocity_x,
        velocity_y,
        velocity_z,
        coord_x * coord_x,
        coord_y * coord_y,
        coord_z * coord_z,
        coord_x * coord_y,
        coord_x * coord_z,
        coord_y * coord_z,
    ]
    feature_blocks = jnp.stack(
        [(weight * jnp.broadcast_to(piece, shape)).reshape(blocks, block) for piece in pieces], 1
    )
    label_blocks = labels.reshape(blocks, block)
    columns = jnp.arange(structures, dtype=jnp.int32)

    def accumulate(total, inputs):
        feature_rows, marks = inputs
        onehot = (marks[:, None] == columns[None, :]).astype(jnp.float32)
        return (total + product(feature_rows, onehot), None)

    partial_sums, unused = lax.scan(
        accumulate, jnp.zeros((13, structures), jnp.float32), (feature_blocks, label_blocks)
    )
    owner_slots = slot_table(structure_owner[0], per_owner)
    parcel_slots = slot_table(parcel_owner[0], per_owner)
    mine_owned = lax.dynamic_slice_in_dim(owner_slots, row_index * per_owner, per_owner, 1)
    totals = lax.psum(partial_sums, "py")
    owned = product(totals, mine_owned)
    mine_parcels = lax.dynamic_slice_in_dim(parcel_slots, row_index * per_owner, per_owner, 1)
    received = product(parcel_rows(totals), mine_parcels)
    return (remaining, owned[None], received[None])


def solution(mesh):
    return jax.shard_map(
        local,
        mesh=mesh,
        in_specs=(
            P("px", "py", None),
            P("px", "py", None),
            P("px", "py", None),
            P("px", "py", None),
            P("px", "py", None),
            P("px", None),
            P("px", None),
        ),
        out_specs=(P("px", "py", None), P("px", None, "py"), P("px", None, "py")),
        check_vma=False,
    )
```

profile of v0, /device:TPU:0, one launch (start us, length us, event | category | flops | bytes accessed | tf_op | source)
XLA Modules:
  0.0 86.4 jit_solution(18232538209815463961)
XLA Ops:
  0.7 0.9 %pad_maximum_fusion.7 = (f32[2,2,8,640]{3,2,1,0:T(8,128)S(1)}, f32[2,2,8,640]{3,2,1,0:T(8,128)S(1)}) fusion(f32[1,8,8,640]{3,2,1,0:T(8,128)} %bitcast.59, f32[1,8,8,640]{3,2,1,0:T(8,128)} %bitcast.63), kind=kLoop, calls=%fused_computation.82 | loop fusion | flops 40960 | bytes 491520 | tf_op jit(solution)/shard_map/stack | solution.py:74
  1.6 2.5 %collective-permute-start.1 = (f32[2,2,8,640]{3,2,1,0:T(8,128)S(1)}, f32[2,2,8,640]{3,2,1,0:T(8,128)S(1)}, u32[]{:S(2)}, u32[]{:S(2)}) collective-permute-start(f32[2,2,8,640]{3,2,1,0:T(8,128)S(1)} %get-tuple-element.72), channel_id=1, source_target_pairs={{8,0},{16,8},{24,16},{0,24},{9,1},{17,9},{25,17},{1,25},{10,2},{18... | collective-permute-start | bytes 245768 | tf_op jit(solution)/shard_map/ppermute | solution.py:17
  4.2 1.7 %reshape.154 = s32[10,4096]{1,0:T(8,128)} reshape(s32[8,8,640]{2,1,0:T(8,128)} %param.13) | data formatting | bytes 327680 | tf_op jit(solution)/shard_map/reshape | solution.py:120
  5.9 0.9 %convert_reduce_fusion = s32[32]{0:T(128)S(1)} fusion(s32[32]{0:T(128)} %bitcast.70), kind=kLoop, calls=%fused_computation.112 | loop fusion | flops 5088 | bytes 256 | tf_op jit(solution)/shard_map/reduce_sum | solution.py:63
  6.8 0.7 multiply_add_fusion
  7.5 0.9 %convert_reduce_fusion.1 = s32[32]{0:T(128)S(1)} fusion(s32[32]{0:T(128)} %bitcast.71), kind=kLoop, calls=%fused_computation.113 | loop fusion | flops 5088 | bytes 256 | tf_op jit(solution)/shard_map/reduce_sum | solution.py:63
  8.4 0.7 multiply_add_fusion.1
  9.0 1.2 %pad_maximum_fusion.1 = (f32[2,10,8,640]{3,2,1,0:T(8,128)S(1)}, f32[2,10,8,640]{3,2,1,0:T(8,128)S(1)}) fusion(f32[2,2,8,640]{3,2,1,0:T(8,128)S(1)} %collective-permute-done.1, f32[1,8,8,640]{3,2,1,0:T(8,128)} %bitcast.60, f32[1,8,8,640]{3,2,1,0:T(8,128)} %bitcast.64, f32[2,2,8,640]{3,2,1,0:T(8,128)S(1)} %collective-permute-done), kind=kLoop, calls=%fused_computation.12 | loop fusion | flops 409600 | bytes 1310720 | tf_op jit(solution)/shard_map/concatenate | solution.py:18
  10.3 1.0 %fusion.16 = f32[10,8,640]{2,1,0:T(8,128)S(1)} fusion(f32[2,10,8,640]{3,2,1,0:T(8,128)S(1)} %get-tuple-element.71, f32[2,10,8,640]{3,2,1,0:T(8,128)S(1)} %get-tuple-element.70, f32[2,2,8,640]{3,2,1,0:T(8,128)S(1)} %collective-permute-done.1, f32[1,8,8,640]{3,2,1,0:T(8,128)} %bitcast.61, f32[1,8,8,640]{3,2,1,0:T(8,128)} %bitcast.65, ...), kind=kLoop, calls=%fused_computation.42 | loop fusion | flops 563200 | bytes 1105920 | tf_op jit(solution)/shard_map/min | solution.py:30
  11.5 3.4 %collective-permute-start.2 = (f32[2,8,2,640]{3,2,1,0:T(2,128)S(1)}, f32[2,8,2,640]{3,2,1,0:T(2,128)S(1)}, u32[]{:S(2)}, u32[]{:S(2)}) collective-permute-start(f32[2,8,2,640]{3,2,1,0:T(2,128)S(1)} %get-tuple-element.68), channel_id=1, source_target_pairs={{0,1},{1,2},{2,3},{3,4},{4,5},{5,6},{6,7},{8,9},{9,10},{10,11},{11... | collective-permute-start | bytes 245768 | tf_op jit(solution)/shard_map/ppermute | solution.py:16
  14.9 1.3 %collective-permute-start.3 = (f32[2,8,2,640]{3,2,1,0:T(2,128)S(1)}, f32[2,8,2,640]{3,2,1,0:T(2,128)S(1)}, u32[]{:S(2)}, u32[]{:S(2)}) collective-permute-start(f32[2,8,2,640]{3,2,1,0:T(2,128)S(1)} %get-tuple-element.69), channel_id=1, source_target_pairs={{1,0},{2,1},{3,2},{4,3},{5,4},{6,5},{7,6},{9,8},{10,9},{11,10},{12... | collective-permute-start | bytes 245768 | tf_op jit(solution)/shard_map/ppermute | solution.py:17
  16.2 1.3 %collective-permute-done.2 = f32[2,8,2,640]{3,2,1,0:T(2,128)S(1)} collective-permute-done((f32[2,8,2,640]{3,2,1,0:T(2,128)S(1)}, f32[2,8,2,640]{3,2,1,0:T(2,128)S(1)}, u32[]{:S(2)}, u32[]{:S(2)}) %collective-permute-start.2) | collective-permute-done | bytes 81952 | tf_op jit(solution)/shard_map/ppermute | solution.py:16
  17.5 4.1 %collective-permute-done.3 = f32[2,8,2,640]{3,2,1,0:T(2,128)S(1)} collective-permute-done((f32[2,8,2,640]{3,2,1,0:T(2,128)S(1)}, f32[2,8,2,640]{3,2,1,0:T(2,128)S(1)}, u32[]{:S(2)}, u32[]{:S(2)}) %collective-permute-start.3) | collective-permute-done | bytes 81952 | tf_op jit(solution)/shard_map/ppermute | solution.py:17
  21.9 0.2 fusion.6
  22.2 0.2 fusion.23
  22.4 0.2 fusion.19
  22.8 0.9 %broadcast_multiply_fusion.1 = (f32[8,8,640]{2,1,0:T(8,128)S(1)}, f32[8,8,640]{2,1,0:T(8,128)S(1)}, f32[8,8,640]{2,1,0:T(8,128)S(1)}, f32[8,8,640]{2,1,0:T(8,128...) fusion(f32[8,8,640]{2,1,0:T(8,128)S(1)} %get-tuple-element.65, ...), kind=kLoop, calls=%fused_computation.85 | loop fusion | flops 819200 | bytes 3302784 | tf_op jit(solution)/shard_map/mul | solution.py:118
  23.7 0.7 constant_dynamic-update-slice_fusion.12
  25.0 0.7 constant_dynamic-update-slice_fusion.11
  25.7 0.7 constant_dynamic-update-slice_fusion.10
  26.4 0.7 constant_dynamic-update-slice_fusion.9
  27.2 0.7 constant_dynamic-update-slice_fusion.8
  27.9 0.7 constant_dynamic-update-slice_fusion.7
  28.6 0.7 constant_dynamic-update-slice_fusion.6
  29.4 0.7 constant_dynamic-update-slice_fusion.5
  30.1 0.7 constant_dynamic-update-slice_fusion.4
  30.8 0.7 constant_dynamic-update-slice_fusion.3
  31.6 0.7 constant_dynamic-update-slice_fusion.2
  32.3 0.7 constant_dynamic-update-slice_fusion.1
  33.0 0.7 constant_dynamic-update-slice_fusion
  33.7 30.6 %while.11 = (s32[]{:T(128)}, f32[13,32]{1,0:T(8,128)S(1)}, f32[10,13,4096]{2,0,1:T(8,128)}, s32[10,4096]{1,0:T(8,128)}, s32[]{:T(128)}, /*index=5*/s32[]{:T(128)}) while((s32[]{:T(128)}, f32[13,32]{1,0:T(8,128)S(1)}, f32[10,13,4096]{2,0,1:T(8,128)}, s32[10,4096]{1,0:T(8,128)}, s32[]{:T(128)}, /*index=5*/s32[]{:T(128)}) %tuple.55), condition=%wide.region_1.2_spmd.clone, body=%wide.region_0.1_spmd.clone.sunk | while | flops 20579140 | bytes 691543 | solution.py:128
  33.7 1.6 %constant_dynamic-slice_fusion.4 = f32[1,13,4096]{2,0,1:T(1,128)S(1)} fusion(f32[10,13,4096]{2,0,1:T(8,128)} %get-tuple-element.143, s32[]{:T(128)} %get-tuple-element.135), kind=kLoop, calls=%fused_computation.6.clone.1 | loop fusion | bytes 425988 | tf_op jit(solution)/shard_map/while/body/jit(dynamic_index_in_dim)/dynamic_slice | solution.py:128
  35.4 0.9 %constant_dynamic-slice_fusion.5 = s32[1,4096]{1,0:T(1,128)S(1)} fusion(s32[10,4096]{1,0:T(8,128)} %get-tuple-element.144, s32[]{:T(128)} %get-tuple-element.135), kind=kLoop, calls=%fused_computation.5.clone.1 | loop fusion | bytes 32772 | tf_op jit(solution)/shard_map/while/body/jit(dynamic_index_in_dim)/dynamic_slice | solution.py:128
  36.3 0.5 convolution_add_fusion.2
  36.8 1.6 %constant_dynamic-slice_fusion.4 = f32[1,13,4096]{2,0,1:T(1,128)S(1)} fusion(f32[10,13,4096]{2,0,1:T(8,128)} %get-tuple-element.143, s32[]{:T(128)} %get-tuple-element.135), kind=kLoop, calls=%fused_computation.6.clone.1 | loop fusion | bytes 425988 | tf_op jit(solution)/shard_map/while/body/jit(dynamic_index_in_dim)/dynamic_slice | solution.py:128
  38.5 0.9 %constant_dynamic-slice_fusion.5 = s32[1,4096]{1,0:T(1,128)S(1)} fusion(s32[10,4096]{1,0:T(8,128)} %get-tuple-element.144, s32[]{:T(128)} %get-tuple-element.135), kind=kLoop, calls=%fused_computation.5.clone.1 | loop fusion | bytes 32772 | tf_op jit(solution)/shard_map/while/body/jit(dynamic_index_in_dim)/dynamic_slice | solution.py:128
  39.4 0.5 convolution_add_fusion.2
  39.9 1.6 %constant_dynamic-slice_fusion.4 = f32[1,13,4096]{2,0,1:T(1,128)S(1)} fusion(f32[10,13,4096]{2,0,1:T(8,128)} %get-tuple-element.143, s32[]{:T(128)} %get-tuple-element.135), kind=kLoop, calls=%fused_computation.6.clone.1 | loop fusion | bytes 425988 | tf_op jit(solution)/shard_map/while/body/jit(dynamic_index_in_dim)/dynamic_slice | solution.py:128
  41.5 0.9 %constant_dynamic-slice_fusion.5 = s32[1,4096]{1,0:T(1,128)S(1)} fusion(s32[10,4096]{1,0:T(8,128)} %get-tuple-element.144, s32[]{:T(128)} %get-tuple-element.135), kind=kLoop, calls=%fused_computation.5.clone.1 | loop fusion | bytes 32772 | tf_op jit(solution)/shard_map/while/body/jit(dynamic_index_in_dim)/dynamic_slice | solution.py:128
  42.5 0.5 convolution_add_fusion.2
  42.9 1.6 %constant_dynamic-slice_fusion.4 = f32[1,13,4096]{2,0,1:T(1,128)S(1)} fusion(f32[10,13,4096]{2,0,1:T(8,128)} %get-tuple-element.143, s32[]{:T(128)} %get-tuple-element.135), kind=kLoop, calls=%fused_computation.6.clone.1 | loop fusion | bytes 425988 | tf_op jit(solution)/shard_map/while/body/jit(dynamic_index_in_dim)/dynamic_slice | solution.py:128
  44.6 0.9 %constant_dynamic-slice_fusion.5 = s32[1,4096]{1,0:T(1,128)S(1)} fusion(s32[10,4096]{1,0:T(8,128)} %get-tuple-element.144, s32[]{:T(128)} %get-tuple-element.135), kind=kLoop, calls=%fused_computation.5.clone.1 | loop fusion | bytes 32772 | tf_op jit(solution)/shard_map/while/body/jit(dynamic_index_in_dim)/dynamic_slice | solution.py:128
  45.5 0.5 convolution_add_fusion.2
  46.0 1.6 %constant_dynamic-slice_fusion.4 = f32[1,13,4096]{2,0,1:T(1,128)S(1)} fusion(f32[10,13,4096]{2,0,1:T(8,128)} %get-tuple-element.143, s32[]{:T(128)} %get-tuple-element.135), kind=kLoop, calls=%fused_computation.6.clone.1 | loop fusion | bytes 425988 | tf_op jit(solution)/shard_map/while/body/jit(dynamic_index_in_dim)/dynamic_slice | solution.py:128
  47.7 0.9 %constant_dynamic-slice_fusion.5 = s32[1,4096]{1,0:T(1,128)S(1)} fusion(s32[10,4096]{1,0:T(8,128)} %get-tuple-element.144, s32[]{:T(128)} %get-tuple-element.135), kind=kLoop, calls=%fused_computation.5.clone.1 | loop fusion | bytes 32772 | tf_op jit(solution)/shard_map/while/body/jit(dynamic_index_in_dim)/dynamic_slice | solution.py:128
  48.6 0.5 convolution_add_fusion.2
  49.1 1.6 %constant_dynamic-slice_fusion.4 = f32[1,13,4096]{2,0,1:T(1,128)S(1)} fusion(f32[10,13,4096]{2,0,1:T(8,128)} %get-tuple-element.143, s32[]{:T(128)} %get-tuple-element.135), kind=kLoop, calls=%fused_computation.6.clone.1 | loop fusion | bytes 425988 | tf_op jit(solution)/shard_map/while/body/jit(dynamic_index_in_dim)/dynamic_slice | solution.py:128
  50.7 0.9 %constant_dynamic-slice_fusion.5 = s32[1,4096]{1,0:T(1,128)S(1)} fusion(s32[10,4096]{1,0:T(8,128)} %get-tuple-element.144, s32[]{:T(128)} %get-tuple-element.135), kind=kLoop, calls=%fused_computation.5.clone.1 | loop fusion | bytes 32772 | tf_op jit(solution)/shard_map/while/body/jit(dynamic_index_in_dim)/dynamic_slice | solution.py:128
  51.7 0.5 convolution_add_fusion.2
  52.1 1.6 %constant_dynamic-slice_fusion.4 = f32[1,13,4096]{2,0,1:T(1,128)S(1)} fusion(f32[10,13,4096]{2,0,1:T(8,128)} %get-tuple-element.143, s32[]{:T(128)} %get-tuple-element.135), kind=kLoop, calls=%fused_computation.6.clone.1 | loop fusion | bytes 425988 | tf_op jit(solution)/shard_map/while/body/jit(dynamic_index_in_dim)/dynamic_slice | solution.py:128
  53.8 0.9 %constant_dynamic-slice_fusion.5 = s32[1,4096]{1,0:T(1,128)S(1)} fusion(s32[10,4096]{1,0:T(8,128)} %get-tuple-element.144, s32[]{:T(128)} %get-tuple-element.135), kind=kLoop, calls=%fused_computation.5.clone.1 | loop fusion | bytes 32772 | tf_op jit(solution)/shard_map/while/body/jit(dynamic_index_in_dim)/dynamic_slice | solution.py:128
  54.7 0.5 convolution_add_fusion.2
  55.2 1.6 %constant_dynamic-slice_fusion.4 = f32[1,13,4096]{2,0,1:T(1,128)S(1)} fusion(f32[10,13,4096]{2,0,1:T(8,128)} %get-tuple-element.143, s32[]{:T(128)} %get-tuple-element.135), kind=kLoop, calls=%fused_computation.6.clone.1 | loop fusion | bytes 425988 | tf_op jit(solution)/shard_map/while/body/jit(dynamic_index_in_dim)/dynamic_slice | solution.py:128
  56.9 0.9 %constant_dynamic-slice_fusion.5 = s32[1,4096]{1,0:T(1,128)S(1)} fusion(s32[10,4096]{1,0:T(8,128)} %get-tuple-element.144, s32[]{:T(128)} %get-tuple-element.135), kind=kLoop, calls=%fused_computation.5.clone.1 | loop fusion | bytes 32772 | tf_op jit(solution)/shard_map/while/body/jit(dynamic_index_in_dim)/dynamic_slice | solution.py:128
  57.8 0.5 convolution_add_fusion.2
  58.3 1.6 %constant_dynamic-slice_fusion.4 = f32[1,13,4096]{2,0,1:T(1,128)S(1)} fusion(f32[10,13,4096]{2,0,1:T(8,128)} %get-tuple-element.143, s32[]{:T(128)} %get-tuple-element.135), kind=kLoop, calls=%fused_computation.6.clone.1 | loop fusion | bytes 425988 | tf_op jit(solution)/shard_map/while/body/jit(dynamic_index_in_dim)/dynamic_slice | solution.py:128
  59.9 0.9 %constant_dynamic-slice_fusion.5 = s32[1,4096]{1,0:T(1,128)S(1)} fusion(s32[10,4096]{1,0:T(8,128)} %get-tuple-element.144, s32[]{:T(128)} %get-tuple-element.135), kind=kLoop, calls=%fused_computation.5.clone.1 | loop fusion | bytes 32772 | tf_op jit(solution)/shard_map/while/body/jit(dynamic_index_in_dim)/dynamic_slice | solution.py:128
  60.9 0.5 convolution_add_fusion.2
  61.3 1.6 %constant_dynamic-slice_fusion.4 = f32[1,13,4096]{2,0,1:T(1,128)S(1)} fusion(f32[10,13,4096]{2,0,1:T(8,128)} %get-tuple-element.143, s32[]{:T(128)} %get-tuple-element.135), kind=kLoop, calls=%fused_computation.6.clone.1 | loop fusion | bytes 425988 | tf_op jit(solution)/shard_map/while/body/jit(dynamic_index_in_dim)/dynamic_slice | solution.py:128
  63.0 0.9 %constant_dynamic-slice_fusion.5 = s32[1,4096]{1,0:T(1,128)S(1)} fusion(s32[10,4096]{1,0:T(8,128)} %get-tuple-element.144, s32[]{:T(128)} %get-tuple-element.135), kind=kLoop, calls=%fused_computation.5.clone.1 | loop fusion | bytes 32772 | tf_op jit(solution)/shard_map/while/body/jit(dynamic_index_in_dim)/dynamic_slice | solution.py:128
  63.9 0.5 convolution_add_fusion.2
  64.4 20.1 %psum.7 = f32[13,32]{1,0:T(8,128)S(1)} all-reduce(f32[13,32]{1,0:T(8,128)S(1)} %get-tuple-element.30), channel_id=1, replica_groups=mesh['px'=4,'py'=8] {'py'}, use_global_device_ids=true, to_apply=%region_2.3 | all-reduce | flops 416 | bytes 3328 | tf_op jit(solution)/shard_map/psum | solution.py:134
  84.6 0.8 convolution_bitcast_fusion.1
  85.5 0.8 convolution_bitcast_fusion
  (46 shorter events, 1.5 us)
Async XLA Ops:
  0.6 10.6 %copy-start.1 = (f32[8,8,640]{2,1,0:T(8,128)S(1)}, f32[8,8,640]{2,1,0:T(8,128)}, u32[]{:S(2)}) copy-start(f32[8,8,640]{2,1,0:T(8,128)} %param.9) | copy-start | bytes 491524
  0.6 10.6 %copy-start = (f32[8,8,640]{2,1,0:T(8,128)S(1)}, f32[8,8,640]{2,1,0:T(8,128)}, u32[]{:S(2)}) copy-start(f32[8,8,640]{2,1,0:T(8,128)} %param.10) | copy-start | bytes 491524
  0.7 10.8 %copy-start.4 = (f32[8,8,640]{2,1,0:T(8,128)S(1)}, f32[8,8,640]{2,1,0:T(8,128)}, u32[]{:S(2)}) copy-start(f32[8,8,640]{2,1,0:T(8,128)} %param.11) | copy-start | bytes 491524
  1.6 7.5 %collective-permute-start.1 = (f32[2,2,8,640]{3,2,1,0:T(8,128)S(1)}, f32[2,2,8,640]{3,2,1,0:T(8,128)S(1)}, u32[]{:S(2)}, u32[]{:S(2)}) collective-permute-start(f32[2,2,8,640]{3,2,1,0:T(8,128)S(1)} %get-tuple-element.72), channel_id=1, source_target_pairs={{8,0},{16,8},{24,16},{0,24},{9,1},{17,9},{25,17},{1,25},{10,2},{18... | collective-permute-start | bytes 245768 | tf_op jit(solution)/shard_map/ppermute | solution.py:17
  4.0 5.0 %collective-permute-start = (f32[2,2,8,640]{3,2,1,0:T(8,128)S(1)}, f32[2,2,8,640]{3,2,1,0:T(8,128)S(1)}, u32[]{:S(2)}, u32[]{:S(2)}) collective-permute-start(f32[2,2,8,640]{3,2,1,0:T(8,128)S(1)} %get-tuple-element.73), channel_id=1, source_target_pairs={{0,8},{8,16},{16,24},{24,0},{1,9},{9,17},{17,25},{25,1},{2,10},{10... | collective-permute-start | bytes 245768 | tf_op jit(solution)/shard_map/ppermute | solution.py:16
  11.5 6.0 %collective-permute-start.2 = (f32[2,8,2,640]{3,2,1,0:T(2,128)S(1)}, f32[2,8,2,640]{3,2,1,0:T(2,128)S(1)}, u32[]{:S(2)}, u32[]{:S(2)}) collective-permute-start(f32[2,8,2,640]{3,2,1,0:T(2,128)S(1)} %get-tuple-element.68), channel_id=1, source_target_pairs={{0,1},{1,2},{2,3},{3,4},{4,5},{5,6},{6,7},{8,9},{9,10},{10,11},{11... | collective-permute-start | bytes 245768 | tf_op jit(solution)/shard_map/ppermute | solution.py:16
  14.9 6.7 %collective-permute-start.3 = (f32[2,8,2,640]{3,2,1,0:T(2,128)S(1)}, f32[2,8,2,640]{3,2,1,0:T(2,128)S(1)}, u32[]{:S(2)}, u32[]{:S(2)}) collective-permute-start(f32[2,8,2,640]{3,2,1,0:T(2,128)S(1)} %get-tuple-element.69), channel_id=1, source_target_pairs={{1,0},{2,1},{3,2},{4,3},{5,4},{6,5},{7,6},{9,8},{10,9},{11,10},{12... | collective-permute-start | bytes 245768 | tf_op jit(solution)/shard_map/ppermute | solution.py:17
  16.2 6.2 %copy-start.2 = (f32[8,8,640]{2,1,0:T(8,128)S(1)}, f32[8,8,640]{2,1,0:T(8,128)}, u32[]{:S(2)}) copy-start(f32[8,8,640]{2,1,0:T(8,128)} %param.12) | copy-start | bytes 491524
  21.8 1.0 %copy-start.3 = (s32[8,8,640]{2,1,0:T(8,128)S(1)}, s32[8,8,640]{2,1,0:T(8,128)}, u32[]{:S(2)}) copy-start(s32[8,8,640]{2,1,0:T(8,128)} %param.13) | copy-start | bytes 491524
where the time goes:
time: 87.1 us; the launch traced here: 86.4 us
  local copies, waits for them, and re-layouts  37.5 us (43%)
  blocking collectives  20.1 us (23%)
  other arithmetic  8.61 us (10%)
  starting transfers between devices  7.18 us (8%)
  matrix products  6.3 us (7%)
  waiting for transfers between devices  5.37 us (6%)
  between operations  0.97 us (1%)
    dynamic_slice x20, local copies, waits for them, and re-layouts, local(): lax.scan(accumulate, jnp.zeros((13, structures), jnp.float32), (feature_b...  25.7 us
    psum x1, blocking collectives, local(): totals = lax.psum(partial_sums, 'py')  20.1 us
    unnamed x22, local copies, waits for them, and re-layouts  8.8 us
    dot_general x12, matrix products, product(): jnp.dot(left, right, precision=lax.Precision.HIGHEST, preferred_element_t...  6.3 us
    ppermute x2, waiting for transfers between devices, with_halo(): after = lax.ppermute(initial, axis, down)  4.12 us
    ppermute x2, starting transfers between devices, with_halo(): after = lax.ppermute(initial, axis, down)  3.75 us
    ppermute x2, starting transfers between devices, with_halo(): before = lax.ppermute(last, axis, up)  3.43 us
    reduce_sum x2, other arithmetic, slot_table(): rank = jnp.sum((same & earlier).astype(jnp.int32), axis=1)  1.82 us
  transfers between devices with their start and end apart: 4, of which 2 were waited for; matrix products, arithmetic and copies ran while one was open for 6% of the time, Pallas kernels for 0%

commit v1 on v0

v1 whole, which is shorter than its diff:
```python
import functools

import jax
import jax.numpy as jnp
from jax import lax
from jax.experimental import pallas as pl
from jax.experimental.pallas import tpu as pltpu
from jax.sharding import PartitionSpec as P

MESH = pl.DeviceIdType.MESH
FEATURES = 9


def slope_of(before, centre, after):
    bound = 2.0 * jnp.minimum(centre, 1.0 - centre)
    return jnp.minimum(jnp.maximum(0.5 * (after - before), -bound), bound)


def flux_of(courant, f_low, s_low, f_high, s_high):
    positive = courant > 0.0
    donor = jnp.where(positive, f_low, f_high)
    slope = jnp.where(positive, s_low, -s_high)
    return courant * (donor + 0.5 * (1.0 - jnp.abs(courant)) * slope)


def slot_row(owner, per_owner):
    count = owner.shape[1]
    rows = lax.broadcasted_iota(jnp.int32, (count, count), 0)
    columns = lax.broadcasted_iota(jnp.int32, (count, count), 1)
    wide = jnp.broadcast_to(owner, (count, count)).astype(jnp.float32)
    column = jnp.sum(jnp.where(rows == columns, wide, 0.0), axis=1, keepdims=True)
    earlier = (wide == column) & (rows < columns)
    rank = jnp.sum(jnp.where(earlier, 1.0, 0.0), axis=0, keepdims=True)
    return owner.astype(jnp.float32) * per_owner + rank


def kernel(
    n_px, n_py,
    f_in, cx_in, cy_in, cz_in, lab_in, so_ref, po_ref,
    rem_out, mom_ref, par_ref,
    p_ref, h_ref, c_ref, ch_ref, cy_ref, cyh_ref, cz_ref, lab_ref, hot_ref, acc_ref,
    rem_ref, row_ref, part_ref, slots_ref,
    local_sem, halo_send, halo_recv, part_send, part_recv,
):
    size_x, size_y, depth = f_in.shape
    structures = so_ref.shape[1]
    per_owner = structures // n_py
    px = lax.axis_index("px")
    py = lax.axis_index("py")
    has_low = py > 0
    has_high = py < n_py - 1

    loads = [
        (lab_in, lab_ref),
        (f_in, p_ref.at[pl.ds(2, size_x)]),
        (cx_in, c_ref.at[pl.ds(1, size_x)]),
        (cy_in, cy_ref),
        (cz_in, cz_ref),
    ]
    copies = [pltpu.make_async_copy(s, d, local_sem.at[k]) for k, (s, d) in enumerate(loads)]
    for copy in copies:
        copy.start()

    def device(dx, dy):
        return (lax.rem(px + dx + n_px, n_px), py + dy)

    barrier = pltpu.get_barrier_semaphore()

    def greet(where):
        pl.semaphore_signal(barrier, inc=1, device_id=where, device_id_type=MESH)

    def peer(step):
        return lax.rem(py + step, n_py)

    for step in range(1, n_py):
        greet((px, peer(step)))
    for dx in (-1, 1):
        greet(device(dx, 0))

    @pl.when(has_low)
    def _():
        greet(device(-1, -1))
        greet(device(1, -1))

    @pl.when(has_high)
    def _():
        greet(device(-1, 1))
        greet(device(1, 1))

    callers = n_py + 1 + jnp.where(has_low, 2, 0) + jnp.where(has_high, 2, 0)
    pl.semaphore_wait(barrier, callers)

    end_x, end_y = size_x - 2, size_y - 2
    last_x, low, high = pl.ds(size_x - 1, 1), pl.ds(end_y, 2), pl.ds(0, 2)
    all_x, all_c = pl.ds(2, size_x), pl.ds(1, size_x)
    top_f, bottom_f = pl.ds(end_x, 2), pl.ds(0, 2)
    beyond = pl.ds(size_x + 2, 2)
    moves = []
    for dy, rows in ((1, low), (-1, high)):
        moves.append((f_in.at[top_f, rows], h_ref.at[pl.ds(0, 2), rows], 1, dy))
        moves.append((f_in.at[bottom_f, rows], h_ref.at[beyond, rows], -1, dy))
        moves.append((cx_in.at[last_x, rows], ch_ref.at[pl.ds(0, 1), rows], 1, dy))
    for dy, rows in ((1, low), (-1, high)):
        moves.append((f_in.at[:, rows], h_ref.at[all_x, rows], 0, dy))
        moves.append((cx_in.at[:, rows], ch_ref.at[all_c, rows], 0, dy))
    last_y = pl.ds(size_y - 1, 1)
    moves.append((cy_in.at[:, last_y], cyh_ref.at[:, last_y], 0, 1))
    moves.append((f_in.at[top_f], p_ref.at[pl.ds(0, 2)], 1, 0))
    moves.append((cx_in.at[last_x], c_ref.at[pl.ds(0, 1)], 1, 0))
    moves.append((f_in.at[bottom_f], p_ref.at[beyond], -1, 0))

    remote = [
        pltpu.make_async_remote_copy(
            src_ref=source, dst_ref=target, send_sem=halo_send.at[k], recv_sem=halo_recv.at[k],
            device_id=device(dx, dy), device_id_type=MESH,
        )
        for k, (source, target, dx, dy) in enumerate(moves)
    ]

    def for_rows(dy, action):
        chosen = [copy for copy, move in zip(remote, moves) if move[3] == dy]

        def run():
            for copy in chosen:
                action(copy)

        if dy == 0:
            run()
        else:
            sends = action is start_copy or action is wait_sent
            pl.when(has_high if (dy > 0) == sends else has_low)(run)

    def start_copy(copy):
        copy.start()

    def wait_sent(copy):
        copy.wait_send()

    def wait_arrived(copy):
        copy.wait_recv()

    for dy in (1, -1, 0):
        for_rows(dy, start_copy)

    copies[0].wait()
    names = lax.broadcasted_iota(jnp.int32, (structures, depth), 0)

    def mark(i, carry):
        for j in range(size_y):
            line = jnp.broadcast_to(lab_ref[i, pl.ds(j, 1), :], (structures, depth))
            hot = jnp.where(line == names, 1.0, 0.0).astype(jnp.bfloat16)
            hot_ref[i, pl.ds(j * structures, structures), :] = hot
        return carry

    lax.fori_loop(0, size_x, mark, 0)
    owned_slots = slot_row(so_ref[...], per_owner)
    parcel_slots = slot_row(po_ref[...], per_owner)

    for copy in copies[1:]:
        copy.wait()
    for dy in (1, -1, 0):
        for_rows(dy, wait_arrived)

    plane = (size_y, depth)
    sub = lax.broadcasted_iota(jnp.int32, plane, 0)
    lane = lax.broadcasted_iota(jnp.int32, plane, 1)
    first_row, last_row = sub == 0, sub == size_y - 1
    first_cell, last_cell = lane == 0, lane == depth - 1
    low_limit = jnp.where(has_low, end_y, size_y)
    high_limit = jnp.where(has_high, 2, 0)
    halo_valid = (sub >= low_limit) | (sub < high_limit)
    coord_z = (lane.astype(jnp.float32) + 0.5) / depth
    scale = 4.0 / (size_x * size_y * size_y)

    def next_y(main, other):
        return pltpu.roll(jnp.where(first_row, other, main), size_y - 1, 0)

    def prior_y(main, other):
        return pltpu.roll(jnp.where(last_row, other, main), 1, 0)

    def next_z(value):
        return jnp.where(last_cell, 0.0, pltpu.roll(value, depth - 1, 1))

    def prior_z(value):
        return jnp.where(first_cell, 0.0, pltpu.roll(value, 1, 1))

    class Along:
        def __init__(self, frac, cour):
            self.frac, self.cour = frac, cour
            before = slope_of(frac[0], frac[1], frac[2])
            self.slope = slope_of(frac[1], frac[2], frac[3])
            self.flux = flux_of(cour[0], frac[1], before, frac[2], self.slope)

        def layer(self, i):
            frac, here, below = self.frac[i + 2], self.cour[i + 1], self.cour[i]
            later = self.frac[i + 3]
            slope = slope_of(frac, later, self.frac[i + 4])
            flux = flux_of(here, frac, self.slope, later, slope)
            result = frac - (flux - self.flux) + frac * (here - below)
            self.slope, self.flux = slope, flux
            return result, 0.5 * (here + below)

    main_x, halo_x = Along(p_ref, c_ref), Along(h_ref, ch_ref)
    for i in range(size_x):
        first, velocity_x = main_x.layer(i)
        outer, _ = halo_x.layer(i)
        outer = jnp.where(halo_valid, outer, 0.0)

        c = cy_ref[i]
        c_outer = jnp.where(halo_valid, cyh_ref[i], 0.0)
        after, after_outer = next_y(first, outer), next_y(outer, first)
        slope = slope_of(prior_y(first, outer), first, after)
        slope_outer = slope_of(prior_y(outer, first), outer, after_outer)
        flux = flux_of(c, first, slope, after, next_y(slope, slope_outer))
        flux_outer = flux_of(c_outer, outer, slope_outer, after_outer, next_y(slope_outer, slope))
        below = prior_y(c, c_outer)
        second = first - (flux - prior_y(flux, flux_outer)) + first * (c - below)
        velocity_y = 0.5 * (c + below)

        c = cz_ref[i]
        after = next_z(second)
        slope = slope_of(prior_z(second), second, after)
        flux = flux_of(c, second, slope, after, next_z(slope))
        below = prior_z(c)
        third = second - (flux - prior_z(flux)) + second * (c - below)
        velocity_z = 0.5 * (c + below)

        rem_ref[i] = jnp.where(lab_ref[i] >= 0, 0.0, third)
        coord_x = ((px * size_x + i).astype(jnp.float32) + 0.5) / (size_x * n_px)
        w = third * scale
        wx, wz = w * coord_x, w * coord_z
        features = [w, wx, wx * coord_x, wz, wx * coord_z, wz * coord_z,
                    w * velocity_x, w * velocity_y, w * velocity_z]
        parts = []
        for value in features:
            parts.append(value)
            parts.append(value - value.astype(jnp.bfloat16).astype(jnp.float32))
        left = jnp.concatenate(parts, axis=0).astype(jnp.bfloat16)
        sums = lax.dot_general(left, hot_ref[i], (((1,), (1,)), ((), ())),
                               preferred_element_type=jnp.float32)
        if i == 0:
            acc_ref[...] = sums
        else:
            acc_ref[...] += sums

    store = pltpu.make_async_copy(rem_ref, rem_out, local_sem.at[len(loads)])
    store.start()

    width = size_y * structures
    sub = lax.broadcasted_iota(jnp.int32, (size_y, width), 0)
    lane = lax.broadcasted_iota(jnp.int32, (size_y, width), 1)
    mine = (lane >= sub * structures) & (lane < (sub + 1) * structures)
    coord_y = ((py * size_y + sub).astype(jnp.float32) + 0.5) / (size_y * n_py)

    def collect(k):
        base = 2 * size_y * k
        both = acc_ref[pl.ds(base, size_y), :] + acc_ref[pl.ds(base + size_y, size_y), :]
        return jnp.where(mine, both, 0.0)

    def put(row, value):
        row_ref[pl.ds(row, 1), :] = jnp.sum(value, axis=0, keepdims=True)

    row_ref[...] = jnp.zeros_like(row_ref)
    w, wx, wxx, wz, wxz, wzz, ux, uy, uz = [collect(k) for k in range(FEATURES)]
    wy = w * coord_y
    for row, value in enumerate((w, wx, wy, wz, ux, uy, uz, wxx, wy * coord_y, wzz,
                                 wx * coord_y, wxz, wz * coord_y)):
        put(row, value)
    total = row_ref[:, pl.ds(0, structures)]
    for j in range(1, size_y):
        total = total + row_ref[:, pl.ds(j * structures, structures)]
    part_ref[...] = total
    slots_ref[py] = total

    sends = []
    for step in range(1, n_py):
        copy = pltpu.make_async_remote_copy(
            src_ref=part_ref, dst_ref=slots_ref.at[py],
            send_sem=part_send.at[step], recv_sem=part_recv.at[py],
            device_id=(px, peer(step)), device_id_type=MESH,
        )
        copy.start()
        sends.append(copy)
    for dy in (1, -1, 0):
        for_rows(dy, wait_sent)
    for step in range(1, n_py):
        source = peer(step)
        pltpu.make_async_remote_copy(
            src_ref=part_ref, dst_ref=slots_ref.at[source],
            send_sem=part_send.at[step], recv_sem=part_recv.at[source],
            device_id=(px, source), device_id_type=MESH,
        ).wait_recv()

    total = slots_ref[0]
    for k in range(1, n_py):
        total = total + slots_ref[k]

    def pick(slots):
        where = lax.broadcasted_iota(jnp.int32, (total.shape[0], per_owner), 1)
        result = jnp.zeros((total.shape[0], per_owner), jnp.float32)
        for j in range(per_owner):
            chosen = slots == (py * per_owner + j).astype(jnp.float32)
            column = jnp.sum(jnp.where(chosen, total, 0.0), axis=1, keepdims=True)
            result = jnp.where(where == j, column, result)
        return result

    mom_ref[0] = pick(owned_slots)[:13]
    m = pick(parcel_slots)
    volume = m[0:1]
    safe = jnp.maximum(volume, 0.5)
    centre = m[1:4] / safe
    velocity = m[4:7] / safe
    square = m[7:10] / safe - centre * centre
    par_ref[0, 0:1] = volume
    par_ref[0, 1:4] = centre
    par_ref[0, 4:7] = velocity
    par_ref[0, 7:10] = square
    par_ref[0, 10:11] = m[10:11] / safe - centre[0:1] * centre[1:2]
    par_ref[0, 11:12] = m[11:12] / safe - centre[0:1] * centre[2:3]
    par_ref[0, 12:13] = m[12:13] / safe - centre[1:2] * centre[2:3]

    store.wait()
    for copy in sends:
        copy.wait_send()


def local(n_px, n_py, fraction, courant_x, courant_y, courant_z, labels, structure_owner, parcel_owner):
    size_x, size_y, depth = fraction.shape
    structures = structure_owner.shape[1]
    per_owner = structures // n_py
    f32 = jnp.float32
    block = (size_x, size_y, depth)
    rows = 16
    moves = 14
    any_spec = pl.BlockSpec(memory_space=pl.ANY)
    vmem = pl.BlockSpec(memory_space=pltpu.VMEM)
    dma = pltpu.SemaphoreType.DMA
    return pl.pallas_call(
        functools.partial(kernel, n_px, n_py),
        out_shape=(
            jax.ShapeDtypeStruct(block, f32),
            jax.ShapeDtypeStruct((1, 13, per_owner), f32),
            jax.ShapeDtypeStruct((1, 13, per_owner), f32),
        ),
        in_specs=[any_spec] * 5 + [vmem] * 2,
        out_specs=(any_spec, vmem, vmem),
        scratch_shapes=[
            pltpu.VMEM((size_x + 4, size_y, depth), f32),
            pltpu.VMEM((size_x + 4, size_y, depth), f32),
            pltpu.VMEM((size_x + 1, size_y, depth), f32),
            pltpu.VMEM((size_x + 1, size_y, depth), f32),
            pltpu.VMEM(block, f32),
            pltpu.VMEM(block, f32),
            pltpu.VMEM(block, f32),
            pltpu.VMEM(block, jnp.int32),
            pltpu.VMEM((size_x, size_y * structures, depth), jnp.bfloat16),
            pltpu.VMEM((FEATURES * 2 * size_y, size_y * structures), f32),
            pltpu.VMEM(block, f32),
            pltpu.VMEM((rows, size_y * structures), f32),
            pltpu.VMEM((rows, structures), f32),
            pltpu.VMEM((n_py, rows, structures), f32),
            dma((6,)),
            dma((moves,)),
            dma((moves,)),
            dma((n_py,)),
            dma((n_py,)),
        ],
        compiler_params=pltpu.CompilerParams(collective_id=0, has_side_effects=True),
    )(fraction, courant_x, courant_y, courant_z, labels, structure_owner, parcel_owner)


def solution(mesh):
    return jax.shard_map(
        functools.partial(local, mesh.shape["px"], mesh.shape["py"]),
        mesh=mesh,
        in_specs=(P("px", "py", None),) * 5 + (P("px", None),) * 2,
        out_specs=(P("px", "py", None), P("px", None, "py"), P("px", None, "py")),
        check_vma=False,
    )
```

time: 87.1 us -> 24.6 us (0.28)
  local copies, waits for them, and re-layouts: 37.5 us -> 3.61 us
  Pallas kernels: 0 us -> 20.1 us
  blocking collectives: 20.1 us -> 0 us
  other arithmetic: 8.61 us -> 0 us
  starting transfers between devices: 7.18 us -> 0 us
  matrix products: 6.3 us -> 0 us
  waiting for transfers between devices: 5.37 us -> 0 us
    dynamic_slice x20 -> x0, local copies, waits for them, and re-layouts: 25.7 us -> none  [local(): lax.scan(accumulate, jnp.zeros((13, structures), jnp.float32), (feature_b...]
    psum x1 -> x0, blocking collectives: 20.1 us -> none  [local(): totals = lax.psum(partial_sums, 'py')]
    pallas_call x0 -> x1, Pallas kernels: none -> 20.1 us  [local(): pl.pallas_call(functools.partial(kernel, n_px, n_py), out_shape=(jax.Shap...]
    unnamed x22 -> x3, local copies, waits for them, and re-layouts: 8.8 us -> 1.6 us
    ppermute x4 -> x0, starting transfers between devices: 7.18 us -> none  [the longest x2 3.75 us: with_halo(): after = lax.ppermute(initial, axis, down)]
    dot_general x12 -> x0, matrix products: 6.3 us -> none  [product(): jnp.dot(left, right, precision=lax.Precision.HIGHEST, preferred_element_t...]
    ppermute x4 -> x0, waiting for transfers between devices: 5.37 us -> none  [the longest x2 4.12 us: with_halo(): after = lax.ppermute(initial, axis, down)]
    pallas_call x0 -> x2, local copies, waits for them, and re-layouts: none -> 2.02 us  [local(): pl.pallas_call(functools.partial(kernel, n_px, n_py), out_shape=(jax.Shap...]
  transfers between devices with their start and end apart: 4 -> 0, of which waited for: 2 -> 0; matrix products, arithmetic and copies ran while one was open for 6% -> 0% of each run, Pallas kernels for 0% -> 0%
where the time goes in v1:
time: 24.6 us; the launch traced here: 24.4 us
  Pallas kernels  20.1 us (82%)
  local copies, waits for them, and re-layouts  3.61 us (15%)
  between operations  0.65 us (3%)
    pallas_call x1, Pallas kernels, local(): pl.pallas_call(functools.partial(kernel, n_px, n_py), out_shape=(jax.Shap...  20.1 us
    pallas_call x2, local copies, waits for them, and re-layouts, local(): pl.pallas_call(functools.partial(kernel, n_px, n_py), out_shape=(jax.Shap...  2.02 us
    unnamed x3, local copies, waits for them, and re-layouts  1.6 us

profile of v1, /device:TPU:0, one launch (start us, length us, event | category | flops | bytes accessed | tf_op | source)
XLA Modules:
  0.0 24.4 jit_solution(13862656516357322563)
XLA Ops:
  0.6 20.1 %shard_map.94 = (f32[8,8,640]{2,1,0:T(8,128)}, f32[1,13,4]{2,1,0:T(8,128)}, f32[1,13,4]{2,1,0:T(8,128)}) custom-call(f32[8,8,640]{2,1,0:T(8,128)} %f_in.1, f32[8,8,640]{2,1,0:T(8,128)} %cx_in.1, f32[8,8,640]{2,1,0:T(8,128)} %cy_in.1, f32[8,8,640]{2,1,0:T(8,128)} %cz_in.1, s32[8,8,640]{2,1,0:T(8,128)} %lab_in.1, s32[1,32]{1,0:T(1,128)} %so_ref.1, s32[1,32]{1,0:T(1,128)} %po_ref.1), custom_call_target="tpu_custom_call" | custom-call | tf_op jit(solution)/shard_map/pallas_call | solution.py:338
  20.7 0.0 copy-start
  20.7 1.4 %copy.10 = f32[1,13,4]{1,2,0:T(4,128)} copy(f32[1,13,4]{2,1,0:T(8,128)} %get-tuple-element.4) | data formatting | bytes 416 | tf_op jit(solution)/shard_map/pallas_call | solution.py:338
  22.1 0.0 copy-done
  22.1 0.7 %copy.11 = f32[1,13,4]{1,2,0:T(4,128)} copy(f32[1,13,4]{2,1,0:T(8,128)S(1)} %copy-done) | data formatting | bytes 416 | tf_op jit(solution)/shard_map/pallas_call | solution.py:338
  22.8 1.6 %copy.13 = f32[8,8,640]{2,1,0:T(8,128)} copy(f32[8,8,640]{2,1,0:T(8,128)} %get-tuple-element.9) | data formatting | bytes 327680
Async XLA Ops:
  20.7 1.4 %copy-start = (f32[1,13,4]{2,1,0:T(8,128)S(1)}, f32[1,13,4]{2,1,0:T(8,128)}, u32[]{:S(2)}) copy-start(f32[1,13,4]{2,1,0:T(8,128)} %get-tuple-element.5) | copy-start | bytes 628

commit v2 on v1

--- a/solution.py
+++ b/solution.py
@@ -9,6 +9,7 @@
 
 MESH = pl.DeviceIdType.MESH
 FEATURES = 9
+ROWS = 16
 
 
 def slope_of(before, centre, after):
@@ -34,21 +35,76 @@
     return owner.astype(jnp.float32) * per_owner + rank
 
 
+def pack_groups(structures):
+    return 128 // structures if structures < 128 and 128 % structures == 0 and structures >= 8 else 1
+
+
+def packed(row_ref, structures):
+    width = row_ref.shape[1]
+    groups = pack_groups(structures)
+    if groups == 1 or width % 128:
+        total = row_ref[:, pl.ds(0, structures)]
+        for j in range(1, width // structures):
+            total = total + row_ref[:, pl.ds(j * structures, structures)]
+        if groups == 1:
+            return total
+        total = jnp.concatenate([total] * groups, axis=1)
+    else:
+        total = row_ref[:, pl.ds(0, 128)]
+        for j in range(1, width // 128):
+            total = total + row_ref[:, pl.ds(j * 128, 128)]
+        shift = 64
+        while shift >= structures:
+            total = total + pltpu.roll(total, shift, 1)
+            shift //= 2
+    rows = ROWS // groups
+    lane = lax.broadcasted_iota(jnp.int32, (rows, 128), 1)
+    result = total[:rows]
+    for k in range(1, groups):
+        result = jnp.where(lane >= k * structures, total[k * rows : (k + 1) * rows], result)
+    return result
+
+
 def kernel(
     n_px, n_py,
-    f_in, cx_in, cy_in, cz_in, lab_in, so_ref, po_ref,
-    rem_out, mom_ref, par_ref,
+    structures,
+    f_in, cx_in, cy_in, cz_in, lab_in, so_in, po_in,
+    rem_ref, total_ref, place_ref,
     p_ref, h_ref, c_ref, ch_ref, cy_ref, cyh_ref, cz_ref, lab_ref, hot_ref, acc_ref,
-    rem_ref, row_ref, part_ref, slots_ref,
+    row_ref, part_ref, slots_ref, so_ref, po_ref,
     local_sem, halo_send, halo_recv, part_send, part_recv,
 ):
     size_x, size_y, depth = f_in.shape
-    structures = so_ref.shape[1]
-    per_owner = structures // n_py
     px = lax.axis_index("px")
     py = lax.axis_index("py")
     has_low = py > 0
     has_high = py < n_py - 1
+
+    def device(dx, dy):
+        return (lax.rem(px + dx + n_px, n_px), py + dy)
+
+    barrier = pltpu.get_barrier_semaphore()
+
+    def greet(where):
+        pl.semaphore_signal(barrier, inc=1, device_id=where, device_id_type=MESH)
+
+    def peer(step):
+        return lax.rem(py + step, n_py)
+
+    for step in range(1, n_py):
+        greet((px, peer(step)))
+    for dx in (-1, 1):
+        greet(device(dx, 0))
+
+    @pl.when(has_low)
+    def _():
+        greet(device(-1, -1))
+        greet(device(1, -1))
+
+    @pl.when(has_high)
+    def _():
+        greet(device(-1, 1))
+        greet(device(1, 1))
 
     loads = [
         (lab_in, lab_ref),
@@ -56,36 +112,12 @@
         (cx_in, c_ref.at[pl.ds(1, size_x)]),
         (cy_in, cy_ref),
         (cz_in, cz_ref),
+        (so_in, so_ref),
+        (po_in, po_ref),
     ]
     copies = [pltpu.make_async_copy(s, d, local_sem.at[k]) for k, (s, d) in enumerate(loads)]
     for copy in copies:
         copy.start()
-
-    def device(dx, dy):
-        return (lax.rem(px + dx + n_px, n_px), py + dy)
-
-    barrier = pltpu.get_barrier_semaphore()
-
-    def greet(where):
-        pl.semaphore_signal(barrier, inc=1, device_id=where, device_id_type=MESH)
-
-    def peer(step):
-        return lax.rem(py + step, n_py)
-
-    for step in range(1, n_py):
-        greet((px, peer(step)))
-    for dx in (-1, 1):
-        greet(device(dx, 0))
-
-    @pl.when(has_low)
-    def _():
-        greet(device(-1, -1))
-        greet(device(1, -1))
-
-    @pl.when(has_high)
-    def _():
-        greet(device(-1, 1))
-        greet(device(1, 1))
 
     callers = n_py + 1 + jnp.where(has_low, 2, 0) + jnp.where(has_high, 2, 0)
     pl.semaphore_wait(barrier, callers)
@@ -153,11 +185,11 @@
         return carry
 
     lax.fori_loop(0, size_x, mark, 0)
-    owned_slots = slot_row(so_ref[...], per_owner)
-    parcel_slots = slot_row(po_ref[...], per_owner)
 
     for copy in copies[1:]:
         copy.wait()
+    place_ref[0:1] = slot_row(so_ref[...], structures // n_py)
+    place_ref[1:2] = slot_row(po_ref[...], structures // n_py)
     for dy in (1, -1, 0):
         for_rows(dy, wait_arrived)
 
@@ -243,9 +275,6 @@
         else:
             acc_ref[...] += sums
 
-    store = pltpu.make_async_copy(rem_ref, rem_out, local_sem.at[len(loads)])
-    store.start()
-
     width = size_y * structures
     sub = lax.broadcasted_iota(jnp.int32, (size_y, width), 0)
     lane = lax.broadcasted_iota(jnp.int32, (size_y, width), 1)
@@ -266,9 +295,7 @@
     for row, value in enumerate((w, wx, wy, wz, ux, uy, uz, wxx, wy * coord_y, wzz,
                                  wx * coord_y, wxz, wz * coord_y)):
         put(row, value)
-    total = row_ref[:, pl.ds(0, structures)]
-    for j in range(1, size_y):
-        total = total + row_ref[:, pl.ds(j * structures, structures)]
+    total = packed(row_ref, structures)
     part_ref[...] = total
     slots_ref[py] = total
 
@@ -295,33 +322,39 @@
     for k in range(1, n_py):
         total = total + slots_ref[k]
 
-    def pick(slots):
-        where = lax.broadcasted_iota(jnp.int32, (total.shape[0], per_owner), 1)
-        result = jnp.zeros((total.shape[0], per_owner), jnp.float32)
-        for j in range(per_owner):
-            chosen = slots == (py * per_owner + j).astype(jnp.float32)
-            column = jnp.sum(jnp.where(chosen, total, 0.0), axis=1, keepdims=True)
-            result = jnp.where(where == j, column, result)
-        return result
-
-    mom_ref[0] = pick(owned_slots)[:13]
-    m = pick(parcel_slots)
-    volume = m[0:1]
-    safe = jnp.maximum(volume, 0.5)
-    centre = m[1:4] / safe
-    velocity = m[4:7] / safe
-    square = m[7:10] / safe - centre * centre
-    par_ref[0, 0:1] = volume
-    par_ref[0, 1:4] = centre
-    par_ref[0, 4:7] = velocity
-    par_ref[0, 7:10] = square
-    par_ref[0, 10:11] = m[10:11] / safe - centre[0:1] * centre[1:2]
-    par_ref[0, 11:12] = m[11:12] / safe - centre[0:1] * centre[2:3]
-    par_ref[0, 12:13] = m[12:13] / safe - centre[1:2] * centre[2:3]
-
-    store.wait()
+    total_ref[...] = total
     for copy in sends:
         copy.wait_send()
+
+
+def finish(n_py, rem_in, total_ref, place_ref, rem_out, mom_ref, par_ref, sem):
+    store = pltpu.make_async_copy(rem_in, rem_out, sem)
+    store.start()
+    structures = place_ref.shape[1]
+    per_owner = structures // n_py
+    py = lax.axis_index("py")
+    groups = pack_groups(structures)
+    total = total_ref[...]
+    if groups > 1:
+        total = jnp.concatenate([total[:, k * structures : (k + 1) * structures] for k in range(groups)], axis=0)
+
+    def pick(slots):
+        wanted = lax.broadcasted_iota(jnp.int32, (per_owner, structures), 0) + py * per_owner
+        chosen = jnp.where(slots == wanted.astype(jnp.float32), 1.0, 0.0)
+        return lax.dot_general(chosen, total, (((1,), (1,)), ((), ())),
+                               precision=lax.Precision.HIGHEST, preferred_element_type=jnp.float32)
+
+    mom_ref[0] = pick(place_ref[0:1])[:, :13]
+    m = pick(place_ref[1:2])
+    volume = m[:, 0:1]
+    q = m / jnp.maximum(volume, 0.5)
+    centre = q[:, 1:4]
+    par_ref[0, :, 0:1] = volume
+    par_ref[0, :, 1:7] = q[:, 1:7]
+    par_ref[0, :, 7:10] = q[:, 7:10] - centre * centre
+    par_ref[0, :, 10:12] = q[:, 10:12] - q[:, 1:2] * q[:, 2:4]
+    par_ref[0, :, 12:13] = q[:, 12:13] - q[:, 2:3] * q[:, 3:4]
+    store.wait()
 
 
 def local(n_px, n_py, fraction, courant_x, courant_y, courant_z, labels, structure_owner, parcel_owner):
@@ -330,20 +363,20 @@
     per_owner = structures // n_py
     f32 = jnp.float32
     block = (size_x, size_y, depth)
-    rows = 16
     moves = 14
+    groups = pack_groups(structures)
+    packet = (ROWS // groups, groups * structures)
+    width = size_y * structures
     any_spec = pl.BlockSpec(memory_space=pl.ANY)
     vmem = pl.BlockSpec(memory_space=pltpu.VMEM)
     dma = pltpu.SemaphoreType.DMA
-    return pl.pallas_call(
-        functools.partial(kernel, n_px, n_py),
-        out_shape=(
-            jax.ShapeDtypeStruct(block, f32),
-            jax.ShapeDtypeStruct((1, 13, per_owner), f32),
-            jax.ShapeDtypeStruct((1, 13, per_owner), f32),
-        ),
-        in_specs=[any_spec] * 5 + [vmem] * 2,
-        out_specs=(any_spec, vmem, vmem),
+    limit = 12 * 2**20 + 4 * size_x * width * depth
+    rem, total, place = pl.pallas_call(
+        functools.partial(kernel, n_px, n_py, structures),
+        out_shape=(jax.ShapeDtypeStruct(block, f32), jax.ShapeDtypeStruct(packet, f32),
+                   jax.ShapeDtypeStruct((2, structures), f32)),
+        in_specs=[pl.BlockSpec(memory_space=pltpu.HBM)] * 7,
+        out_specs=(vmem, vmem, vmem),
         scratch_shapes=[
             pltpu.VMEM((size_x + 4, size_y, depth), f32),
             pltpu.VMEM((size_x + 4, size_y, depth), f32),
@@ -353,20 +386,33 @@
             pltpu.VMEM(block, f32),
             pltpu.VMEM(block, f32),
             pltpu.VMEM(block, jnp.int32),
-            pltpu.VMEM((size_x, size_y * structures, depth), jnp.bfloat16),
-            pltpu.VMEM((FEATURES * 2 * size_y, size_y * structures), f32),
-            pltpu.VMEM(block, f32),
-            pltpu.VMEM((rows, size_y * structures), f32),
-            pltpu.VMEM((rows, structures), f32),
-            pltpu.VMEM((n_py, rows, structures), f32),
-            dma((6,)),
+            pltpu.VMEM((size_x, width, depth), jnp.bfloat16),
+            pltpu.VMEM((FEATURES * 2 * size_y, width), f32),
+            pltpu.VMEM((ROWS, width), f32),
+            pltpu.VMEM(packet, f32),
+            pltpu.VMEM((n_py,) + packet, f32),
+            pltpu.VMEM((1, structures), jnp.int32),
+            pltpu.VMEM((1, structures), jnp.int32),
+            dma((7,)),
             dma((moves,)),
             dma((moves,)),
             dma((n_py,)),
             dma((n_py,)),
         ],
-        compiler_params=pltpu.CompilerParams(collective_id=0, has_side_effects=True),
-    )(fraction, courant_x, courant_y, courant_z, labels, structure_owner, parcel_owner)
+        compiler_params=pltpu.CompilerParams(
+            collective_id=0, has_side_effects=True, vmem_limit_bytes=min(limit, 60 * 2**20)),
+    )(*[pltpu.with_memory_space_constraint(x, pltpu.HBM)
+        for x in (fraction, courant_x, courant_y, courant_z, labels, structure_owner, parcel_owner)])
+    small = jax.ShapeDtypeStruct((1, per_owner, 13), f32)
+    rem, moments, parcels = pl.pallas_call(
+        functools.partial(finish, n_py),
+        out_shape=(jax.ShapeDtypeStruct(block, f32), small, small),
+        in_specs=[any_spec, vmem, vmem],
+        out_specs=(any_spec, vmem, vmem),
+        scratch_shapes=[dma(())],
+        compiler_params=pltpu.CompilerParams(vmem_limit_bytes=8 * 2**20),
+    )(rem, total, place)
+    return rem, jnp.swapaxes(moments, 1, 2), jnp.swapaxes(parcels, 1, 2)
 
 
 def solution(mesh):

time: 24.6 us -> 20.5 us (0.83)
  local copies, waits for them, and re-layouts: 3.61 us -> 0 us
  Pallas kernels: 20.1 us -> 19.8 us
    pallas_call x2 -> x0, local copies, waits for them, and re-layouts: 2.02 us -> none  [local(): pl.pallas_call(functools.partial(kernel, n_px, n_py), out_shape=(jax.Shap...]
    unnamed x3 -> x0, local copies, waits for them, and re-layouts: 1.6 us -> none
    pallas_call x1 -> x2, Pallas kernels: 20.1 us -> 19.8 us  [the longest x1 18.5 us: local(): pl.pallas_call(functools.partial(kernel, n_px, n_py, structures), out_sha...]
where the time goes in v2:
time: 20.5 us; the launch traced here: 20.4 us
  Pallas kernels  19.8 us (97%)
  between operations  0.64 us (3%)
    pallas_call x1, Pallas kernels, local(): pl.pallas_call(functools.partial(kernel, n_px, n_py, structures), out_sha...  18.5 us
    pallas_call x1, Pallas kernels, local(): pl.pallas_call(functools.partial(finish, n_py), out_shape=(jax.ShapeDtype...  1.26 us

profile of v2, /device:TPU:0, one launch (start us, length us, event | category | flops | bytes accessed | tf_op | source)
XLA Modules:
  0.0 20.4 jit_solution(15859099056754517735)
XLA Ops:
  0.6 18.5 %shard_map.94 = (f32[8,8,640]{2,1,0:T(8,128)S(1)}, f32[4,128]{1,0:T(4,128)S(1)}, f32[2,32]{1,0:T(2,128)S(1)}) custom-call(f32[8,8,640]{2,1,0:T(8,128)} %f_in.1, f32[8,8,640]{2,1,0:T(8,128)} %cx_in.1, f32[8,8,640]{2,1,0:T(8,128)} %cy_in.1, f32[8,8,640]{2,1,0:T(8,128)} %cz_in.1, s32[8,8,640]{2,1,0:T(8,128)} %lab_in.1, s32[1,32]{1,0:T(1,128)} %so_in.1, ...), custom_call_target="tpu_custom_call" | custom-call | tf_op jit(solution)/shard_map/pallas_call | solution.py:374
  19.1 1.3 %shard_map.95 = (f32[8,8,640]{2,1,0:T(8,128)}, f32[1,4,13]{2,1,0:T(4,128)}, f32[1,4,13]{2,1,0:T(4,128)}) custom-call(f32[8,8,640]{2,1,0:T(8,128)S(1)} %get-tuple-element.9.rem_in, f32[4,128]{1,0:T(4,128)S(1)} %get-tuple-element.10.total_ref, f32[2,32]{1,0:T(2,128)S(1)} %get-tuple-element.11.place_ref), custom_call_target="tpu_custom_call" | custom-call | tf_op jit(solution)/shard_map/pallas_call | solution.py:407

commit v3 on v2

--- a/solution.py
+++ b/solution.py
@@ -10,6 +10,7 @@
 MESH = pl.DeviceIdType.MESH
 FEATURES = 9
 ROWS = 16
+EDGE, REST, INNER, OUTER = range(4)
 
 
 def slope_of(before, centre, after):
@@ -70,7 +71,7 @@
     structures,
     f_in, cx_in, cy_in, cz_in, lab_in, so_in, po_in,
     rem_ref, total_ref, place_ref,
-    p_ref, h_ref, c_ref, ch_ref, cy_ref, cyh_ref, cz_ref, lab_ref, hot_ref, acc_ref,
+    p_ref, ex_ref, exc_ref, first_ref, edge_ref, outer_ref, c_ref, cy_ref, cyh_ref, cz_ref, lab_ref, hot_ref, acc_ref,
     row_ref, part_ref, slots_ref, so_ref, po_ref,
     local_sem, halo_send, halo_recv, part_send, part_recv,
 ):
@@ -91,25 +92,15 @@
     def peer(step):
         return lax.rem(py + step, n_py)
 
+    for dx in (-1, 1):
+        greet(device(dx, 0))
     for step in range(1, n_py):
         greet((px, peer(step)))
-    for dx in (-1, 1):
-        greet(device(dx, 0))
-
-    @pl.when(has_low)
-    def _():
-        greet(device(-1, -1))
-        greet(device(1, -1))
-
-    @pl.when(has_high)
-    def _():
-        greet(device(-1, 1))
-        greet(device(1, 1))
 
     loads = [
-        (lab_in, lab_ref),
         (f_in, p_ref.at[pl.ds(2, size_x)]),
         (cx_in, c_ref.at[pl.ds(1, size_x)]),
+        (lab_in, lab_ref),
         (cy_in, cy_ref),
         (cz_in, cz_ref),
         (so_in, so_ref),
@@ -119,48 +110,47 @@
     for copy in copies:
         copy.start()
 
-    callers = n_py + 1 + jnp.where(has_low, 2, 0) + jnp.where(has_high, 2, 0)
-    pl.semaphore_wait(barrier, callers)
-
     end_x, end_y = size_x - 2, size_y - 2
-    last_x, low, high = pl.ds(size_x - 1, 1), pl.ds(end_y, 2), pl.ds(0, 2)
-    all_x, all_c = pl.ds(2, size_x), pl.ds(1, size_x)
-    top_f, bottom_f = pl.ds(end_x, 2), pl.ds(0, 2)
+    last_x, last_y = pl.ds(size_x - 1, 1), pl.ds(size_y - 1, 1)
+    low, high = pl.ds(end_y, 2), pl.ds(0, 2)
+    top_x, bottom_x, inner_x = pl.ds(end_x, 2), pl.ds(0, 2), pl.ds(2, size_x - 4)
     beyond = pl.ds(size_x + 2, 2)
     moves = []
+    for rows in (low, high):
+        moves.append((f_in.at[top_x, rows], ex_ref.at[bottom_x, rows], 1, 0, EDGE))
+        moves.append((f_in.at[bottom_x, rows], ex_ref.at[pl.ds(2, 2), rows], -1, 0, EDGE))
+        moves.append((cx_in.at[last_x, rows], exc_ref.at[:, rows], 1, 0, EDGE))
+    moves.append((f_in.at[top_x], p_ref.at[bottom_x], 1, 0, REST))
+    moves.append((f_in.at[bottom_x], p_ref.at[beyond], -1, 0, REST))
+    moves.append((cx_in.at[last_x], c_ref.at[pl.ds(0, 1)], 1, 0, REST))
     for dy, rows in ((1, low), (-1, high)):
-        moves.append((f_in.at[top_f, rows], h_ref.at[pl.ds(0, 2), rows], 1, dy))
-        moves.append((f_in.at[bottom_f, rows], h_ref.at[beyond, rows], -1, dy))
-        moves.append((cx_in.at[last_x, rows], ch_ref.at[pl.ds(0, 1), rows], 1, dy))
-    for dy, rows in ((1, low), (-1, high)):
-        moves.append((f_in.at[:, rows], h_ref.at[all_x, rows], 0, dy))
-        moves.append((cx_in.at[:, rows], ch_ref.at[all_c, rows], 0, dy))
-    last_y = pl.ds(size_y - 1, 1)
-    moves.append((cy_in.at[:, last_y], cyh_ref.at[:, last_y], 0, 1))
-    moves.append((f_in.at[top_f], p_ref.at[pl.ds(0, 2)], 1, 0))
-    moves.append((cx_in.at[last_x], c_ref.at[pl.ds(0, 1)], 1, 0))
-    moves.append((f_in.at[bottom_f], p_ref.at[beyond], -1, 0))
+        moves.append((first_ref.at[inner_x, rows], outer_ref.at[inner_x, rows], 0, dy, INNER))
+        moves.append((edge_ref.at[pl.ds(0, 2), rows], outer_ref.at[bottom_x, rows], 0, dy, OUTER))
+        moves.append((edge_ref.at[pl.ds(2, 2), rows], outer_ref.at[top_x, rows], 0, dy, OUTER))
+    moves.append((cy_in.at[:, last_y], cyh_ref.at[:, last_y], 0, 1, INNER))
 
     remote = [
         pltpu.make_async_remote_copy(
             src_ref=source, dst_ref=target, send_sem=halo_send.at[k], recv_sem=halo_recv.at[k],
             device_id=device(dx, dy), device_id_type=MESH,
         )
-        for k, (source, target, dx, dy) in enumerate(moves)
+        for k, (source, target, dx, dy, group) in enumerate(moves)
     ]
 
-    def for_rows(dy, action):
-        chosen = [copy for copy, move in zip(remote, moves) if move[3] == dy]
-
-        def run():
-            for copy in chosen:
-                action(copy)
-
-        if dy == 0:
-            run()
-        else:
-            sends = action is start_copy or action is wait_sent
-            pl.when(has_high if (dy > 0) == sends else has_low)(run)
+    def for_group(group, action):
+        for dy in (0, 1, -1):
+            chosen = [c for c, move in zip(remote, moves) if move[3] == dy and move[4] == group]
+            if not chosen:
+                continue
+
+            def run():
+                for copy in chosen:
+                    action(copy)
+
+            if dy == 0:
+                run()
+            else:
+                pl.when(has_low if (dy > 0) == (action is wait_arrived) else has_high)(run)
 
     def start_copy(copy):
         copy.start()
@@ -171,10 +161,41 @@
     def wait_arrived(copy):
         copy.wait_recv()
 
-    for dy in (1, -1, 0):
-        for_rows(dy, start_copy)
-
-    copies[0].wait()
+    def whole_f(k):
+        return p_ref[k]
+
+    def whole_c(k):
+        return c_ref[k]
+
+    def edge_f(k):
+        return ex_ref[k] if k < 2 else p_ref[k] if k < size_x + 2 else ex_ref[k - size_x]
+
+    def edge_c(k):
+        return exc_ref[0] if k == 0 else c_ref[k]
+
+    def sweep_x(begin, end, f, c):
+        before = slope_of(f(begin), f(begin + 1), f(begin + 2))
+        slope = slope_of(f(begin + 1), f(begin + 2), f(begin + 3))
+        flux = flux_of(c(begin), f(begin + 1), before, f(begin + 2), slope)
+        for i in range(begin, end):
+            frac, later, here = f(i + 2), f(i + 3), c(i + 1)
+            slope_later = slope_of(frac, later, f(i + 4))
+            flux_later = flux_of(here, frac, slope, later, slope_later)
+            yield i, frac - (flux_later - flux) + frac * (here - c(i))
+            slope, flux = slope_later, flux_later
+
+    for copy in copies[:2]:
+        copy.wait()
+    for i, value in sweep_x(2, end_x, whole_f, whole_c):
+        first_ref[i] = value
+
+    callers = n_py + 1
+    pl.semaphore_wait(barrier, callers)
+    for_group(EDGE, start_copy)
+    for_group(INNER, start_copy)
+    for_group(REST, start_copy)
+
+    copies[2].wait()
     names = lax.broadcasted_iota(jnp.int32, (structures, depth), 0)
 
     def mark(i, carry):
@@ -186,12 +207,22 @@
 
     lax.fori_loop(0, size_x, mark, 0)
 
-    for copy in copies[1:]:
+    for_group(EDGE, wait_arrived)
+    for i, value in sweep_x(0, 2, edge_f, edge_c):
+        edge_ref[i] = value
+    for i, value in sweep_x(end_x, size_x, edge_f, edge_c):
+        edge_ref[i - end_x + 2] = value
+    for_group(OUTER, start_copy)
+
+    for copy in copies[3:]:
         copy.wait()
     place_ref[0:1] = slot_row(so_ref[...], structures // n_py)
     place_ref[1:2] = slot_row(po_ref[...], structures // n_py)
-    for dy in (1, -1, 0):
-        for_rows(dy, wait_arrived)
+    for_group(REST, wait_arrived)
+    for begin, end in ((0, 2), (end_x, size_x)):
+        for i, value in sweep_x(begin, end, whole_f, whole_c):
+            first_ref[i] = value
+    for_group(INNER, wait_arrived)
 
     plane = (size_y, depth)
     sub = lax.broadcasted_iota(jnp.int32, plane, 0)
@@ -216,27 +247,13 @@
     def prior_z(value):
         return jnp.where(first_cell, 0.0, pltpu.roll(value, 1, 1))
 
-    class Along:
-        def __init__(self, frac, cour):
-            self.frac, self.cour = frac, cour
-            before = slope_of(frac[0], frac[1], frac[2])
-            self.slope = slope_of(frac[1], frac[2], frac[3])
-            self.flux = flux_of(cour[0], frac[1], before, frac[2], self.slope)
-
-        def layer(self, i):
-            frac, here, below = self.frac[i + 2], self.cour[i + 1], self.cour[i]
-            later = self.frac[i + 3]
-            slope = slope_of(frac, later, self.frac[i + 4])
-            flux = flux_of(here, frac, self.slope, later, slope)
-            result = frac - (flux - self.flux) + frac * (here - below)
-            self.slope, self.flux = slope, flux
-            return result, 0.5 * (here + below)
-
-    main_x, halo_x = Along(p_ref, c_ref), Along(h_ref, ch_ref)
-    for i in range(size_x):
-        first, velocity_x = main_x.layer(i)
-        outer, _ = halo_x.layer(i)
-        outer = jnp.where(halo_valid, outer, 0.0)
+    order = list(range(2, end_x)) + [0, 1, end_x, size_x - 1]
+    for step, i in enumerate(order):
+        if i == 0:
+            for_group(OUTER, wait_arrived)
+        first = first_ref[i]
+        outer = jnp.where(halo_valid, outer_ref[i], 0.0)
+        velocity_x = 0.5 * (c_ref[i + 1] + c_ref[i])
 
         c = cy_ref[i]
         c_outer = jnp.where(halo_valid, cyh_ref[i], 0.0)
@@ -270,7 +287,7 @@
         left = jnp.concatenate(parts, axis=0).astype(jnp.bfloat16)
         sums = lax.dot_general(left, hot_ref[i], (((1,), (1,)), ((), ())),
                                preferred_element_type=jnp.float32)
-        if i == 0:
+        if step == 0:
             acc_ref[...] = sums
         else:
             acc_ref[...] += sums
@@ -308,8 +325,8 @@
         )
         copy.start()
         sends.append(copy)
-    for dy in (1, -1, 0):
-        for_rows(dy, wait_sent)
+    for group in (EDGE, INNER, REST, OUTER):
+        for_group(group, wait_sent)
     for step in range(1, n_py):
         source = peer(step)
         pltpu.make_async_remote_copy(
@@ -363,7 +380,7 @@
     per_owner = structures // n_py
     f32 = jnp.float32
     block = (size_x, size_y, depth)
-    moves = 14
+    moves = 16
     groups = pack_groups(structures)
     packet = (ROWS // groups, groups * structures)
     width = size_y * structures
@@ -379,8 +396,11 @@
         out_specs=(vmem, vmem, vmem),
         scratch_shapes=[
             pltpu.VMEM((size_x + 4, size_y, depth), f32),
-            pltpu.VMEM((size_x + 4, size_y, depth), f32),
-            pltpu.VMEM((size_x + 1, size_y, depth), f32),
+            pltpu.VMEM((4, size_y, depth), f32),
+            pltpu.VMEM((1, size_y, depth), f32),
+            pltpu.VMEM(block, f32),
+            pltpu.VMEM((4, size_y, depth), f32),
+            pltpu.VMEM(block, f32),
             pltpu.VMEM((size_x + 1, size_y, depth), f32),
             pltpu.VMEM(block, f32),
             pltpu.VMEM(block, f32),

time: 20.5 us -> 18.4 us (0.90)
  Pallas kernels: 19.8 us -> 17.6 us
    pallas_call x1, Pallas kernels: 18.5 us -> 16.3 us  [local(): pl.pallas_call(functools.partial(kernel, n_px, n_py, structures), out_sha...]
where the time goes in v3:
time: 18.4 us; the launch traced here: 18.2 us
  Pallas kernels  17.6 us (96%)
  between operations  0.64 us (3%)
    pallas_call x1, Pallas kernels, local(): pl.pallas_call(functools.partial(kernel, n_px, n_py, structures), out_sha...  16.3 us
    pallas_call x1, Pallas kernels, local(): pl.pallas_call(functools.partial(finish, n_py), out_shape=(jax.ShapeDtype...  1.26 us

profile of v3, /device:TPU:0, one launch (start us, length us, event | category | flops | bytes accessed | tf_op | source)
XLA Modules:
  0.0 18.2 jit_solution(16726836707863461147)
XLA Ops:
  0.6 16.3 %shard_map.94 = (f32[8,8,640]{2,1,0:T(8,128)S(1)}, f32[4,128]{1,0:T(4,128)S(1)}, f32[2,32]{1,0:T(2,128)S(1)}) custom-call(f32[8,8,640]{2,1,0:T(8,128)} %f_in.1, f32[8,8,640]{2,1,0:T(8,128)} %cx_in.1, f32[8,8,640]{2,1,0:T(8,128)} %cy_in.1, f32[8,8,640]{2,1,0:T(8,128)} %cz_in.1, s32[8,8,640]{2,1,0:T(8,128)} %lab_in.1, s32[1,32]{1,0:T(1,128)} %so_in.1, ...), custom_call_target="tpu_custom_call" | custom-call | tf_op jit(solution)/shard_map/pallas_call | solution.py:391
  17.0 1.3 %shard_map.95 = (f32[8,8,640]{2,1,0:T(8,128)}, f32[1,4,13]{2,1,0:T(4,128)}, f32[1,4,13]{2,1,0:T(4,128)}) custom-call(f32[8,8,640]{2,1,0:T(8,128)S(1)} %get-tuple-element.9.rem_in, f32[4,128]{1,0:T(4,128)S(1)} %get-tuple-element.10.total_ref, f32[2,32]{1,0:T(2,128)S(1)} %get-tuple-element.11.place_ref), custom_call_target="tpu_custom_call" | custom-call | tf_op jit(solution)/shard_map/pallas_call | solution.py:427

commit v4 on v3

--- a/solution.py
+++ b/solution.py
@@ -73,7 +73,7 @@
     rem_ref, total_ref, place_ref,
     p_ref, ex_ref, exc_ref, first_ref, edge_ref, outer_ref, c_ref, cy_ref, cyh_ref, cz_ref, lab_ref, hot_ref, acc_ref,
     row_ref, part_ref, slots_ref, so_ref, po_ref,
-    local_sem, halo_send, halo_recv, part_send, part_recv,
+    local_sem, halo_send, halo_recv, part_send, part_recv, go_sem,
 ):
     size_x, size_y, depth = f_in.shape
     px = lax.axis_index("px")
@@ -94,8 +94,10 @@
 
     for dx in (-1, 1):
         greet(device(dx, 0))
-    for step in range(1, n_py):
-        greet((px, peer(step)))
+    root = n_py // 2
+    pl.when(has_low)(lambda: greet((px, py - 1)))
+    pl.when(has_high)(lambda: greet((px, py + 1)))
+    pl.when((py < root - 1) | (py > root + 1))(lambda: greet((px, root)))
 
     loads = [
         (f_in, p_ref.at[pl.ds(2, size_x)]),
@@ -117,9 +119,9 @@
     beyond = pl.ds(size_x + 2, 2)
     moves = []
     for rows in (low, high):
-        moves.append((f_in.at[top_x, rows], ex_ref.at[bottom_x, rows], 1, 0, EDGE))
-        moves.append((f_in.at[bottom_x, rows], ex_ref.at[pl.ds(2, 2), rows], -1, 0, EDGE))
-        moves.append((cx_in.at[last_x, rows], exc_ref.at[:, rows], 1, 0, EDGE))
+        moves.append((p_ref.at[pl.ds(size_x, 2), rows], ex_ref.at[bottom_x, rows], 1, 0, EDGE))
+        moves.append((p_ref.at[pl.ds(2, 2), rows], ex_ref.at[pl.ds(2, 2), rows], -1, 0, EDGE))
+        moves.append((c_ref.at[pl.ds(size_x, 1), rows], exc_ref.at[:, rows], 1, 0, EDGE))
     moves.append((f_in.at[top_x], p_ref.at[bottom_x], 1, 0, REST))
     moves.append((f_in.at[bottom_x], p_ref.at[beyond], -1, 0, REST))
     moves.append((cx_in.at[last_x], c_ref.at[pl.ds(0, 1)], 1, 0, REST))
@@ -189,11 +191,17 @@
     for i, value in sweep_x(2, end_x, whole_f, whole_c):
         first_ref[i] = value
 
-    callers = n_py + 1
-    pl.semaphore_wait(barrier, callers)
+    near = 2 + jnp.where(has_low, 1, 0) + jnp.where(has_high, 1, 0)
+    pl.semaphore_wait(barrier, jnp.where(py == root, n_py + 1, near))
     for_group(EDGE, start_copy)
     for_group(INNER, start_copy)
     for_group(REST, start_copy)
+
+    @pl.when(py == root)
+    def _():
+        for step in range(1, n_py):
+            pl.semaphore_signal(go_sem, inc=1, device_id=(px, peer(step)), device_id_type=MESH)
+
 
     copies[2].wait()
     names = lax.broadcasted_iota(jnp.int32, (structures, depth), 0)
@@ -316,6 +324,7 @@
     part_ref[...] = total
     slots_ref[py] = total
 
+    pl.when(py != root)(lambda: pl.semaphore_wait(go_sem, 1))
     sends = []
     for step in range(1, n_py):
         copy = pltpu.make_async_remote_copy(
@@ -418,6 +427,7 @@
             dma((moves,)),
             dma((n_py,)),
             dma((n_py,)),
+            pltpu.SemaphoreType.REGULAR,
         ],
         compiler_params=pltpu.CompilerParams(
             collective_id=0, has_side_effects=True, vmem_limit_bytes=min(limit, 60 * 2**20)),

time: 18.4 us -> 18.2 us (0.989)
  Pallas kernels: 17.6 us -> 17.4 us
where the time goes in v4:
time: 18.2 us; the launch traced here: 18 us
  Pallas kernels  17.4 us (96%)
  between operations  0.64 us (4%)
    pallas_call x1, Pallas kernels, local(): pl.pallas_call(functools.partial(kernel, n_px, n_py, structures), out_sha...  16.1 us
    pallas_call x1, Pallas kernels, local(): pl.pallas_call(functools.partial(finish, n_py), out_shape=(jax.ShapeDtype...  1.26 us

profile of v4, /device:TPU:0, one launch (start us, length us, event | category | flops | bytes accessed | tf_op | source)
XLA Modules:
  0.0 18.0 jit_solution(12086155783621295718)
XLA Ops:
  0.6 16.1 %shard_map.94 = (f32[8,8,640]{2,1,0:T(8,128)S(1)}, f32[4,128]{1,0:T(4,128)S(1)}, f32[2,32]{1,0:T(2,128)S(1)}) custom-call(f32[8,8,640]{2,1,0:T(8,128)} %f_in.1, f32[8,8,640]{2,1,0:T(8,128)} %cx_in.1, f32[8,8,640]{2,1,0:T(8,128)} %cy_in.1, f32[8,8,640]{2,1,0:T(8,128)} %cz_in.1, s32[8,8,640]{2,1,0:T(8,128)} %lab_in.1, s32[1,32]{1,0:T(1,128)} %so_in.1, ...), custom_call_target="tpu_custom_call" | custom-call | tf_op jit(solution)/shard_map/pallas_call | solution.py:400
  16.8 1.3 %shard_map.95 = (f32[8,8,640]{2,1,0:T(8,128)}, f32[1,4,13]{2,1,0:T(4,128)}, f32[1,4,13]{2,1,0:T(4,128)}) custom-call(f32[8,8,640]{2,1,0:T(8,128)S(1)} %get-tuple-element.9.rem_in, f32[4,128]{1,0:T(4,128)S(1)} %get-tuple-element.10.total_ref, f32[2,32]{1,0:T(2,128)S(1)} %get-tuple-element.11.place_ref), custom_call_target="tpu_custom_call" | custom-call | tf_op jit(solution)/shard_map/pallas_call | solution.py:437

commit v5 on v4

--- a/solution.py
+++ b/solution.py
@@ -10,7 +10,7 @@
 MESH = pl.DeviceIdType.MESH
 FEATURES = 9
 ROWS = 16
-EDGE, REST, INNER, OUTER = range(4)
+EDGE_LOW, EDGE_HIGH, REST, INNER, OUTER_LOW, OUTER_HIGH = range(6)
 
 
 def slope_of(before, centre, after):
@@ -119,16 +119,16 @@
     beyond = pl.ds(size_x + 2, 2)
     moves = []
     for rows in (low, high):
-        moves.append((p_ref.at[pl.ds(size_x, 2), rows], ex_ref.at[bottom_x, rows], 1, 0, EDGE))
-        moves.append((p_ref.at[pl.ds(2, 2), rows], ex_ref.at[pl.ds(2, 2), rows], -1, 0, EDGE))
-        moves.append((c_ref.at[pl.ds(size_x, 1), rows], exc_ref.at[:, rows], 1, 0, EDGE))
+        moves.append((p_ref.at[pl.ds(size_x, 2), rows], ex_ref.at[bottom_x, rows], 1, 0, EDGE_LOW))
+        moves.append((p_ref.at[pl.ds(2, 2), rows], ex_ref.at[pl.ds(2, 2), rows], -1, 0, EDGE_HIGH))
+        moves.append((c_ref.at[pl.ds(size_x, 1), rows], exc_ref.at[:, rows], 1, 0, EDGE_LOW))
     moves.append((f_in.at[top_x], p_ref.at[bottom_x], 1, 0, REST))
     moves.append((f_in.at[bottom_x], p_ref.at[beyond], -1, 0, REST))
     moves.append((cx_in.at[last_x], c_ref.at[pl.ds(0, 1)], 1, 0, REST))
     for dy, rows in ((1, low), (-1, high)):
         moves.append((first_ref.at[inner_x, rows], outer_ref.at[inner_x, rows], 0, dy, INNER))
-        moves.append((edge_ref.at[pl.ds(0, 2), rows], outer_ref.at[bottom_x, rows], 0, dy, OUTER))
-        moves.append((edge_ref.at[pl.ds(2, 2), rows], outer_ref.at[top_x, rows], 0, dy, OUTER))
+        moves.append((edge_ref.at[pl.ds(0, 2), rows], outer_ref.at[bottom_x, rows], 0, dy, OUTER_LOW))
+        moves.append((edge_ref.at[pl.ds(2, 2), rows], outer_ref.at[top_x, rows], 0, dy, OUTER_HIGH))
     moves.append((cy_in.at[:, last_y], cyh_ref.at[:, last_y], 0, 1, INNER))
 
     remote = [
@@ -193,7 +193,8 @@
 
     near = 2 + jnp.where(has_low, 1, 0) + jnp.where(has_high, 1, 0)
     pl.semaphore_wait(barrier, jnp.where(py == root, n_py + 1, near))
-    for_group(EDGE, start_copy)
+    for_group(EDGE_LOW, start_copy)
+    for_group(EDGE_HIGH, start_copy)
     for_group(INNER, start_copy)
     for_group(REST, start_copy)
 
@@ -215,12 +216,29 @@
 
     lax.fori_loop(0, size_x, mark, 0)
 
-    for_group(EDGE, wait_arrived)
-    for i, value in sweep_x(0, 2, edge_f, edge_c):
-        edge_ref[i] = value
-    for i, value in sweep_x(end_x, size_x, edge_f, edge_c):
-        edge_ref[i - end_x + 2] = value
-    for_group(OUTER, start_copy)
+    even = lax.rem(px, 2) == 0
+
+    def lower():
+        for_group(EDGE_LOW, wait_arrived)
+        for i, value in sweep_x(0, 2, edge_f, edge_c):
+            edge_ref[i] = value
+        for_group(OUTER_LOW, start_copy)
+
+    def upper():
+        for_group(EDGE_HIGH, wait_arrived)
+        for i, value in sweep_x(end_x, size_x, edge_f, edge_c):
+            edge_ref[i - end_x + 2] = value
+        for_group(OUTER_HIGH, start_copy)
+
+    @pl.when(even)
+    def _():
+        upper()
+        lower()
+
+    @pl.when(jnp.logical_not(even))
+    def _():
+        lower()
+        upper()
 
     for copy in copies[3:]:
         copy.wait()
@@ -255,10 +273,20 @@
     def prior_z(value):
         return jnp.where(first_cell, 0.0, pltpu.roll(value, 1, 1))
 
-    order = list(range(2, end_x)) + [0, 1, end_x, size_x - 1]
-    for step, i in enumerate(order):
-        if i == 0:
-            for_group(OUTER, wait_arrived)
+    bottom, top = [0, 1], [end_x, end_x + 1]
+
+    def await_side(group, chosen):
+        pl.when(chosen)(lambda: for_group(group, wait_arrived))
+
+    for step in range(size_x):
+        k = step - (size_x - 4)
+        if k < 0:
+            i = step + 2
+        else:
+            if k == 0 or k == 2:
+                await_side(OUTER_HIGH, even if k == 0 else jnp.logical_not(even))
+                await_side(OUTER_LOW, even if k == 2 else jnp.logical_not(even))
+            i = jnp.where(even, (top + bottom)[k], (bottom + top)[k])
         first = first_ref[i]
         outer = jnp.where(halo_valid, outer_ref[i], 0.0)
         velocity_x = 0.5 * (c_ref[i + 1] + c_ref[i])
@@ -334,7 +362,7 @@
         )
         copy.start()
         sends.append(copy)
-    for group in (EDGE, INNER, REST, OUTER):
+    for group in (EDGE_LOW, EDGE_HIGH, INNER, REST, OUTER_LOW, OUTER_HIGH):
         for_group(group, wait_sent)
     for step in range(1, n_py):
         source = peer(step)

time: 18.2 us -> 17.3 us (0.951)
  Pallas kernels: 17.4 us -> 16.5 us
    pallas_call x1, Pallas kernels: 16.1 us -> 15.3 us  [local(): pl.pallas_call(functools.partial(kernel, n_px, n_py, structures), out_sha...]
where the time goes in v5:
time: 17.3 us; the launch traced here: 17.2 us
  Pallas kernels  16.5 us (95%)
  between operations  0.64 us (4%)
    pallas_call x1, Pallas kernels, local(): pl.pallas_call(functools.partial(kernel, n_px, n_py, structures), out_sha...  15.3 us
    pallas_call x1, Pallas kernels, local(): pl.pallas_call(functools.partial(finish, n_py), out_shape=(jax.ShapeDtype...  1.26 us

profile of v5, /device:TPU:0, one launch (start us, length us, event | category | flops | bytes accessed | tf_op | source)
XLA Modules:
  0.0 17.2 jit_solution(8043019918092341695)
XLA Ops:
  0.6 15.3 %shard_map.94 = (f32[8,8,640]{2,1,0:T(8,128)S(1)}, f32[4,128]{1,0:T(4,128)S(1)}, f32[2,32]{1,0:T(2,128)S(1)}) custom-call(f32[8,8,640]{2,1,0:T(8,128)} %f_in.1, f32[8,8,640]{2,1,0:T(8,128)} %cx_in.1, f32[8,8,640]{2,1,0:T(8,128)} %cy_in.1, f32[8,8,640]{2,1,0:T(8,128)} %cz_in.1, s32[8,8,640]{2,1,0:T(8,128)} %lab_in.1, s32[1,32]{1,0:T(1,128)} %so_in.1, ...), custom_call_target="tpu_custom_call" | custom-call | tf_op jit(solution)/shard_map/pallas_call | solution.py:428
  15.9 1.3 %shard_map.95 = (f32[8,8,640]{2,1,0:T(8,128)}, f32[1,4,13]{2,1,0:T(4,128)}, f32[1,4,13]{2,1,0:T(4,128)}) custom-call(f32[8,8,640]{2,1,0:T(8,128)S(1)} %get-tuple-element.9.rem_in, f32[4,128]{1,0:T(4,128)S(1)} %get-tuple-element.10.total_ref, f32[2,32]{1,0:T(2,128)S(1)} %get-tuple-element.11.place_ref), custom_call_target="tpu_custom_call" | custom-call | tf_op jit(solution)/shard_map/pallas_call | solution.py:465
